TPU v7x, 512 devices: a whole 4x8x8 slice. The times are simulated.
512 devices in a mesh: dp: 16 (over z, core), ctx: 8 (over x, y_lo), mp: 4 (over y_hi).
Axes of the slice: x: 4, y: 8 (y_hi: 4, y_lo: 2; y = y_hi * 2 + y_lo), z: 8, core: 2. Of those that a mesh axis runs over, the one named last changes fastest.
Arguments:
- queries: bfloat16 [16, 1024, 4096], P('dp', 'ctx', 'mp'), may hold values from -1.6953125 to 1.6953125
- keys: bfloat16 [16, 1024, 4096], P('dp', 'ctx', 'mp'), may hold values from -1.6953125 to 1.6953125
- values: bfloat16 [16, 1024, 4096], P('dp', 'ctx', 'mp'), may hold values from -6 to 6
- cross_queries: bfloat16 [16, 1024, 4096], P('dp', 'ctx', 'mp'), may hold values from -1.6953125 to 1.6953125
- encoded_bank: bfloat16 [16, 64, 64, 896], P('dp', 'ctx'), may hold values from -6 to 6
- key_weight: bfloat16 [896, 4096], P(('dp', 'ctx'), 'mp'), may hold values from -0.1875 to 0.1875
- value_weight: bfloat16 [896, 4096], P(('dp', 'ctx'), 'mp'), may hold values from -0.1875 to 0.1875
- owner_ids: int32 [16, 16, 2], P('dp', 'ctx'), may hold values from 0 to 15, as said below
- unit_ids: int32 [16, 16, 2], P('dp', 'ctx'), may hold values from 0 to 6
- lengths: int32 [16], P('dp'), may hold values from 64 to 1024
Outputs:
- self_core: bfloat16 [16, 1024, 4096], P('dp', 'ctx', 'mp')
- cross_core: bfloat16 [16, 1024, 4096], P('dp', 'ctx', 'mp')
Inputs may be any that keep to these rules, and one draw needn't show every extreme that they name: `owner_ids`: among the 4 neighbours of the spans of one device (aligned blocks of 2 spans), no owner is named more than once.
All inputs are finite; a program needn't handle non-finite values.
Results may differ from a plain program's by a relative error of at most 0.006.
Values may be sent and summed in bfloat16 or wider, within the bound.
No kernel may reach another device: no remote copies, remote signals or barrier semaphores. Data moves between devices by JAX's collectives and lax.ppermute only.
A program may use at most 64 MiB of HBM per device.

v0:
```python
import math

import jax
import jax.numpy as jnp
from jax import lax
from jax.sharding import PartitionSpec as P

HD = 128
SPAN = 64
NBR = 2


def attend_block(totals, query_heads, positions, key_piece, value_piece, start):
    key_count = key_piece.shape[0]
    head_count = query_heads.shape[1]
    key_heads = key_piece.reshape(key_count, head_count, HD)
    value_heads = value_piece.reshape(key_count, head_count, HD)
    block_size = 512
    last_position = positions[-1]
    for offset in range(0, key_count, block_size):
        key_block = key_heads[offset : offset + block_size]
        value_block = value_heads[offset : offset + block_size]
        block_start = start + offset

        def compute(current):
            running_sums, running_totals = current
            scores = jnp.einsum(
                "qhd,khd->hqk", query_heads, key_block, preferred_element_type=jnp.float32
            ) * (1.0 / math.sqrt(HD))
            key_pos = block_start + jnp.arange(block_size, dtype=jnp.int32)
            allowed = key_pos[None, :] <= positions[:, None]
            weights = jnp.where(allowed[None], jnp.exp(scores), 0.0)
            running_sums = running_sums + jnp.einsum(
                "hqk,khd->qhd",
                weights.astype(jnp.bfloat16),
                value_block,
                preferred_element_type=jnp.float32,
            )
            running_totals = running_totals + jnp.transpose(jnp.sum(weights, axis=2))
            return (running_sums, running_totals)

        def keep(current):
            return current

        active = jnp.logical_and(True, block_start <= last_position)
        totals = lax.cond(active, compute, keep, totals)
    return totals


def empty_totals(row_count, head_count):
    return (
        jnp.zeros((row_count, head_count, HD), jnp.float32),
        jnp.zeros((row_count, head_count), jnp.float32),
    )


def local(
    queries,
    keys,
    values,
    cross_queries,
    encoded_bank,
    key_weight,
    value_weight,
    owner_ids,
    unit_ids,
    lengths,
):
    tok_rows = queries.shape[1]
    feature_width = queries.shape[2]
    head_count = feature_width // HD
    span_count = tok_rows // SPAN
    ctx_index = lax.axis_index("ctx")
    dossier_length = lengths[0]
    positions = ctx_index * tok_rows + jnp.arange(tok_rows, dtype=jnp.int32)
    live_rows = positions < dossier_length
    query_heads = queries[0].reshape(tok_rows, head_count, HD)
    totals = attend_block(
        empty_totals(tok_rows, head_count),
        query_heads,
        positions,
        lax.all_gather(keys, "ctx", axis=1, tiled=True)[0],
        lax.all_gather(values, "ctx", axis=1, tiled=True)[0],
        jnp.int32(0),
    )
    self_heads = totals[0] / totals[1][:, :, None]
    self_core = (
        jnp.where(live_rows[:, None, None], self_heads, 0.0)
        .astype(jnp.bfloat16)
        .reshape(1, tok_rows, feature_width)
    )
    dp_count = lax.axis_size("dp")
    request_total = span_count * NBR
    capacity = -(-request_total // dp_count)
    owners_flat = owner_ids[0].reshape(request_total)
    units_flat = unit_ids[0].reshape(request_total)
    request_order = jnp.arange(request_total, dtype=jnp.int32)
    span_starts = positions[::SPAN]
    live_request = jnp.repeat(span_starts < dossier_length, NBR)
    same_owner = (owners_flat[None, :] == owners_flat[:, None]) & (
        request_order[None, :] < request_order[:, None]
    )
    rank_index = jnp.sum(same_owner.astype(jnp.int32), axis=1)
    slot_index = owners_flat * capacity + rank_index
    slot_numbers = jnp.arange(dp_count * capacity, dtype=jnp.int32)
    matches = (slot_index[:, None] == slot_numbers[None, :]) & live_request[:, None]
    requests = (jnp.sum(jnp.where(matches, units_flat[:, None] + 1, 0), axis=0) - 1).reshape(
        dp_count, capacity
    )
    enc_width = encoded_bank.shape[3]
    bank_local = encoded_bank[0]
    unit_total = bank_local.shape[0]
    asked_units = lax.all_to_all(requests, "dp", split_axis=0, concat_axis=0, tiled=True)
    present = asked_units >= 0
    leading = jnp.clip(asked_units, 0, unit_total - 2)
    joined = jnp.concatenate(
        (jnp.take(bank_local, leading, axis=0), jnp.take(bank_local, leading + 1, axis=0)), axis=2
    )
    joined = jnp.where(present[:, :, None, None], joined, jnp.zeros_like(joined))
    received = lax.all_to_all(joined, "dp", split_axis=0, concat_axis=0, tiled=True)
    own_rows = jnp.take(
        received.reshape(dp_count * capacity, 2 * SPAN, enc_width), slot_index, axis=0
    )
    full_key_weight, full_value_weight = (
        lax.all_gather(key_weight, ("dp", "ctx"), axis=0, tiled=True),
        lax.all_gather(value_weight, ("dp", "ctx"), axis=0, tiled=True),
    )
    retrieved = own_rows.reshape(request_total * 2 * SPAN, enc_width)
    key_proj = jnp.dot(retrieved, full_key_weight, preferred_element_type=jnp.float32).reshape(
        span_count, NBR * 2 * SPAN, head_count, HD
    )
    key_scale = lax.rsqrt(jnp.mean(key_proj * key_proj, axis=3, keepdims=True) + 1e-06)
    cross_keys = (key_proj * key_scale).astype(jnp.bfloat16)
    cross_values = (
        jnp.dot(retrieved, full_value_weight, preferred_element_type=jnp.float32)
        .astype(jnp.bfloat16)
        .reshape(span_count, NBR * 2 * SPAN, head_count, HD)
    )
    span_queries = cross_queries[0].reshape(span_count, SPAN, head_count, HD)
    cross_scores = jnp.einsum(
        "cqhd,ckhd->chqk", span_queries, cross_keys, preferred_element_type=jnp.float32
    ) * (1.0 / math.sqrt(HD))
    cross_weights = jnp.exp(cross_scores)
    cross_sums = jnp.einsum(
        "chqk,ckhd->cqhd",
        cross_weights.astype(jnp.bfloat16),
        cross_values,
        preferred_element_type=jnp.float32,
    )
    cross_totals = jnp.transpose(jnp.sum(cross_weights, axis=3), (0, 2, 1))
    cross_heads = (cross_sums / cross_totals[:, :, :, None]).reshape(tok_rows, head_count, HD)
    cross_core = (
        jnp.where(live_rows[:, None, None], cross_heads, 0.0)
        .astype(jnp.bfloat16)
        .reshape(1, tok_rows, feature_width)
    )
    return (self_core, cross_core)


def solution(mesh):
    in_specs = (
        P("dp", "ctx", "mp"),
        P("dp", "ctx", "mp"),
        P("dp", "ctx", "mp"),
        P("dp", "ctx", "mp"),
        P("dp", "ctx", None, None),
        P(("dp", "ctx"), "mp"),
        P(("dp", "ctx"), "mp"),
        P("dp", "ctx", None),
        P("dp", "ctx", None),
        P("dp"),
    )
    out_specs = (P("dp", "ctx", "mp"), P("dp", "ctx", "mp"))
    return jax.shard_map(local, mesh=mesh, in_specs=in_specs, out_specs=out_specs, check_vma=False)
```

profile of v0, /device:TPU:6, one launch (start us, length us, event | category | flops | bytes accessed | tf_op | source)
XLA Modules:
  0.0 928.9 jit_solution(18198151895259171869)
XLA Ops:
  7.2 0.7 all-gather.13.cloned.1.call-update
  8.0 0.7 all-gather.11.cloned.1.call-update
  9.3 0.7 broadcast_add_fusion
  10.1 0.8 reshape_squeeze.16
  11.4 0.7 copy.76
  12.1 10.4 %all-to-all-start = ((s32[16,1,1]{2,1,0:T(1,128)}), s32[16,1,1]{2,1,0:T(1,128)S(1)}, u32[]{:S(2)}, u32[]{:S(2)}) async-start(s32[16,1,1]{2,1,0:T(1,128)} %copy.76), calls=%async_computation | async-start | bytes 16384 | tf_op jit(solution)/shard_map/all_to_all | solution.py:113
  22.6 1.8 copy.69
  24.4 5.7 all-to-all-done
  30.0 0.4 clamp_reduce_fusion
  30.5 0.8 gather_fusion.2
  31.3 1.5 bitcast_select_fusion
  32.8 0.4 compare_reduce_fusion
  33.2 0.9 gather_fusion.1
  34.3 1.2 copy-done.1
  35.6 2.8 maximum_select_fusion
  38.4 4.6 all-to-all-start.1
  43.2 0.9 copy.70
  44.0 0.6 slice.32
  46.1 0.8 copy.68
  47.0 0.5 broadcast_in_dim.132
  47.5 0.7 copy.90
  48.3 0.6 broadcast_bitcast_fusion
  48.9 355.5 %all-gather.13.cloned.1.call-done = bf16[128,7,1024]{2,1,0:T(8,128)(2,1)} async-done(((bf16[1,7,1024]{2,1,0:T(8,128)(2,1)}), bf16[128,7,1024]{2,1,0:T(8,128)(2,1)}) %all-gather.13.cloned.1.call-update) | async-done | bytes 1835024 | tf_op jit(solution)/shard_map/all_gather | solution.py:125
  404.4 2.7 reshape.338
  407.1 2.5 copy.77
  409.6 369.7 %all-gather.11.cloned.1.call-done = bf16[128,7,1024]{2,1,0:T(8,128)(2,1)} async-done(((bf16[1,7,1024]{2,1,0:T(8,128)(2,1)}), bf16[128,7,1024]{2,1,0:T(8,128)(2,1)}) %all-gather.11.cloned.1.call-update) | async-done | bytes 1835024 | tf_op jit(solution)/shard_map/all_gather | solution.py:126
  779.3 3.9 reshape.336
  783.2 61.9 %all-gather.7.cloned.1.call-done = bf16[1,1024,1024]{1,2,0:T(8,128)(2,1)} async-done(((bf16[1,128,1024]{1,2,0:T(8,128)(2,1)}), bf16[1,1024,1024]{1,2,0:T(8,128)(2,1)}) %all-gather.7.cloned.1.call-update) | async-done | bytes 2097168 | tf_op jit(solution)/shard_map/all_gather | solution.py:82
  845.1 58.6 %all-gather.9.cloned.1.call-done = bf16[1,1024,1024]{1,2,0:T(8,128)(2,1)} async-done(((bf16[1,128,1024]{1,2,0:T(8,128)(2,1)}), bf16[1,1024,1024]{1,2,0:T(8,128)(2,1)}) %all-gather.9.cloned.1.call-update) | async-done | bytes 2097168 | tf_op jit(solution)/shard_map/all_gather | solution.py:83
  903.7 1.2 slice-done
  905.0 2.4 conditional.2
  905.1 1.7 fusion
  906.8 0.5 convolution_bitcast_fusion
  907.3 3.4 conditional.3
  907.4 1.4 slice.24
  908.9 0.3 copy-done.2
  909.4 0.7 fusion.8
  910.1 0.6 fusion.10
  911.1 0.8 reshape.303
  911.9 2.7 gather_fusion
  914.9 2.8 fusion.17
  917.7 0.3 copy.91
  918.0 0.3 copy-done.10
  918.5 0.8 copy-done.4
  919.2 1.3 multiply_reduce_fusion
  920.5 0.4 fusion.30
  920.9 0.3 fusion.20
  921.6 0.8 select_convert_fusion
  (63 shorter events, 2.8 us)
Async XLA Ops:
  7.2 23.3 %copy-start = (bf16[1,8,64,896]{3,2,1,0:T(8,128)(2,1)S(1)}, bf16[1,8,64,896]{3,2,1,0:T(8,128)(2,1)}, u32[]{:S(2)}) copy-start(bf16[1,8,64,896]{3,2,1,0:T(8,128)(2,1)} %param.20) | copy-start | bytes 2752516
  7.2 397.3 %all-gather.13.cloned.1.call-start = ((), (), s32[]{:S(2)}) async-start(), calls=%async_computation.5 | async-start | bytes 2113536 | tf_op jit(solution)/shard_map/all_gather | solution.py:125
  7.9 771.4 %all-gather.11.cloned.1.call-start = ((), (), s32[]{:S(2)}) async-start(), calls=%async_computation.4 | async-start | bytes 2113536 | tf_op jit(solution)/shard_map/all_gather | solution.py:126
  12.1 18.0 %all-to-all-start = ((s32[16,1,1]{2,1,0:T(1,128)}), s32[16,1,1]{2,1,0:T(1,128)S(1)}, u32[]{:S(2)}, u32[]{:S(2)}) async-start(s32[16,1,1]{2,1,0:T(1,128)} %copy.76), calls=%async_computation | async-start | bytes 16384 | tf_op jit(solution)/shard_map/all_to_all | solution.py:113
  22.5 822.6 %all-gather.7.cloned.1.call-start = ((), (), s32[]{:S(2)}) async-start(), calls=%async_computation.2 | async-start | bytes 2359296 | tf_op jit(solution)/shard_map/all_gather | solution.py:82
  34.1 1.5 copy-start.1
  38.4 4.7 copy-start.6
  38.4 6.2 copy-start.9
  38.4 7.7 copy-start.7
  38.4 9.1 copy-start.8
  38.4 873.5 %all-to-all-start.1 = ((bf16[16,1,128,896]{3,2,1,0:T(8,128)(2,1)}), bf16[16,1,128,896]{3,2,1,0:T(8,128)(2,1)}, u32[]{:S(2)}, u32[]{:S(2)}) async-start(bf16[16,1,128,896]{3,2,1,0:T(8,128)(2,1)} %maximum_select_fusion), calls=%async_computation.1 | async-start | bytes 7340032 | tf_op jit(solution)/shard_map/all_to_all | solution.py:120
  43.1 860.6 %all-gather.9.cloned.1.call-start = ((), (), s32[]{:S(2)}) async-start(), calls=%async_computation.3 | async-start | bytes 2359296 | tf_op jit(solution)/shard_map/all_gather | solution.py:83
  845.1 58.6 %slice-start.1 = ((bf16[1,1024,1024]{1,2,0:T(8,128)(2,1)}), bf16[1,512,1024]{1,2,0:T(8,128)(2,1)S(1)}, s32[]{:S(2)}) async-start(bf16[1,1024,1024]{1,2,0:T(8,128)(2,1)} %all-gather.7.cloned.1.call-done), calls=%async_computation.7 | async-start | bytes 2097152 | tf_op jit(solution)/shard_map/slice | solution.py:21
  903.7 1.2 slice-start
  907.3 1.9 copy-start.2
  907.3 2.0 copy-start.3
  910.7 4.0 copy-start.11
  917.7 0.6 copy-start.10
  917.7 1.5 copy-start.4
  919.2 1.3 copy-start.5
Sparse Core Ops, SparseCore 0:
  10.1 394.2 all-gather.12
  406.6 372.7 all-gather.10
  781.9 63.1 all-gather.6
  846.9 56.7 all-gather.8
where the time goes:
time: 930 us; the launch traced here: 929 us
  waiting for transfers between devices  853 us (92%)
  local copies, waits for them, and re-layouts  28.4 us (3%)
  between operations  16 us (2%)
  starting transfers between devices  15.2 us (2%)
    all_gather x1, waiting for transfers between devices, local(): lax.all_gather(value_weight, ('dp', 'ctx'), axis=0, tiled=True)  370 us
    all_gather x1, waiting for transfers between devices, local(): lax.all_gather(key_weight, ('dp', 'ctx'), axis=0, tiled=True)  356 us
    all_gather x1, waiting for transfers between devices, local(): lax.all_gather(keys, 'ctx', axis=1, tiled=True)[0]  61.9 us
    all_gather x1, waiting for transfers between devices, local(): lax.all_gather(values, 'ctx', axis=1, tiled=True)[0]  58.6 us
  transfers between devices with their start and end apart: 6, of which 5 were waited for; matrix products, arithmetic and copies ran while one was open for 3% of the time, Pallas kernels for 0%

commit v1 on v0

v1 whole, which is shorter than its diff:
```python
import functools
import math

import jax
import jax.numpy as jnp
from jax import lax
from jax.experimental import pallas as pl
from jax.experimental.pallas import tpu as pltpu
from jax.sharding import Mesh, PartitionSpec as P

HD = 128
SPAN = 64
NBR = 2
SCALE = 1.0 / math.sqrt(HD)
BF = jnp.bfloat16
F32 = jnp.float32
NT = (((1,), (1,)), ((), ()))


def pack_body(q_ref, k_ref, v_ref, o_ref):
    for h in range(o_ref.shape[0]):
        cols = slice(h * HD, (h + 1) * HD)
        o_ref[h, 0] = q_ref[0, :, cols]
        o_ref[h, 1] = k_ref[0, :, cols]
        o_ref[h, 2] = v_ref[0, :, cols]


def pack_heads(q, k, v):
    rows, width = q.shape[1:]
    return pl.pallas_call(
        pack_body,
        out_shape=jax.ShapeDtypeStruct((width // HD, 3, rows, HD), q.dtype),
        name="pack_heads",
    )(q, k, v)


def self_body(len_ref, x_ref, o_ref, k_ref, v_ref):
    blocks, _, rows, _ = x_ref.shape
    for j in range(blocks):
        k_ref[pl.ds(j * rows, rows), :] = x_ref[j, 1]
        v_ref[pl.ds(j * rows, rows), :] = x_ref[j, 2]
    length = len_ref[0]
    for i in range(blocks):
        width = (i + 1) * rows
        scores = lax.dot_general(
            x_ref[i, 0], k_ref[:width, :], NT, preferred_element_type=F32
        ) * SCALE
        row = lax.broadcasted_iota(jnp.int32, (rows, width), 0) + i * rows
        col = lax.broadcasted_iota(jnp.int32, (rows, width), 1)
        weights = jnp.where(col <= row, jnp.exp(scores), 0.0)
        sums = jnp.dot(weights.astype(BF), v_ref[:width, :], preferred_element_type=F32)
        result = sums / jnp.sum(weights, axis=1, keepdims=True)
        place = lax.broadcasted_iota(jnp.int32, (rows, HD), 0) + i * rows
        o_ref[i] = jnp.where(place < length, result, 0.0).astype(BF)


def self_attention(lengths, x):
    blocks, _, rows, _ = x.shape
    return pl.pallas_call(
        self_body,
        out_shape=jax.ShapeDtypeStruct((blocks, rows, HD), BF),
        in_specs=[
            pl.BlockSpec(memory_space=pltpu.SMEM),
            pl.BlockSpec(memory_space=pltpu.VMEM),
        ],
        scratch_shapes=[pltpu.VMEM((blocks * rows, HD), BF)] * 2,
        name="self_attention",
    )(lengths, x)


def offer_body(ids_ref, where_ref, bank_ref, o_ref, sem, *, asks):
    peers, part = o_ref.shape[0], o_ref.shape[1]
    me, piece = where_ref[0], where_ref[1]
    copies = []
    for r in range(peers):
        unit = jnp.int32(0)
        for t in range(asks):
            unit = jnp.where(ids_ref[r, t] == me, ids_ref[r, asks + t], unit)
        start = pl.multiple_of(unit * SPAN + piece * part, part)
        copies.append(
            pltpu.make_async_copy(bank_ref.at[pl.ds(start, part), :], o_ref.at[r], sem.at[r])
        )
        copies[-1].start()
    for copy in copies:
        copy.wait()


def offer_rows(ids, where, bank, part):
    peers, width = ids.shape
    return pl.pallas_call(
        functools.partial(offer_body, asks=width // 2),
        out_shape=jax.ShapeDtypeStruct((peers, part, bank.shape[1]), bank.dtype),
        in_specs=[
            pl.BlockSpec(memory_space=pltpu.SMEM),
            pl.BlockSpec(memory_space=pltpu.SMEM),
            pl.BlockSpec(memory_space=pl.ANY),
        ],
        out_specs=pl.BlockSpec(memory_space=pltpu.VMEM),
        scratch_shapes=[pltpu.SemaphoreType.DMA((peers,))],
        name="offer_rows",
    )(ids, where, bank)


def choose_body(own_ref, x_ref, o_ref, sem):
    copies = []
    for t in range(o_ref.shape[0]):
        copies.append(pltpu.make_async_copy(x_ref.at[own_ref[t]], o_ref.at[t], sem.at[t]))
        copies[-1].start()
    for copy in copies:
        copy.wait()


def choose_rows(owners, received):
    asks = owners.shape[0]
    return pl.pallas_call(
        choose_body,
        out_shape=jax.ShapeDtypeStruct((asks,) + received.shape[1:], received.dtype),
        in_specs=[
            pl.BlockSpec(memory_space=pltpu.SMEM),
            pl.BlockSpec(memory_space=pl.ANY),
        ],
        out_specs=pl.BlockSpec(memory_space=pltpu.VMEM),
        scratch_shapes=[pltpu.SemaphoreType.DMA((asks,))],
        name="choose_rows",
    )(owners, received)


def cross_body(
    pos_ref, r_ref, pick_ref, ka_ref, kb_ref, va_ref, vb_ref, q_ref, o_ref, rows_ref, *, parts
):
    spans = q_ref.shape[1] // SPAN
    total = r_ref.shape[0]
    half = pick_ref.shape[2]

    @pl.when(pl.program_id(0) == 0)
    def _():
        for side in range(2):
            rows_ref[:, side * half : (side + 1) * half] = jnp.dot(
                r_ref[...], pick_ref[side], preferred_element_type=F32
            ).astype(BF)

    def project(a_ref, b_ref):
        return jnp.dot(rows_ref[:, :half], a_ref[...], preferred_element_type=F32) + jnp.dot(
            rows_ref[:, half:], b_ref[...], preferred_element_type=F32
        )

    key_proj = project(ka_ref, kb_ref)
    value_proj = project(va_ref, vb_ref).astype(BF)
    start, length = pos_ref[0], pos_ref[1]
    for h in range(o_ref.shape[2] // HD):
        cols = slice(h * HD, (h + 1) * HD)
        keys = key_proj[:, cols]
        scale = lax.rsqrt(jnp.mean(keys * keys, axis=1, keepdims=True) + 1e-06)
        keys = (keys * scale).astype(BF).reshape(parts, spans, total // (parts * spans), HD)
        values = value_proj[:, cols].reshape(parts, spans, total // (parts * spans), HD)
        for s in range(spans):
            scores = lax.dot_general(
                q_ref[0, s * SPAN : (s + 1) * SPAN, cols],
                keys[:, s].reshape(total // spans, HD),
                NT,
                preferred_element_type=F32,
            ) * SCALE
            weights = jnp.exp(scores)
            sums = jnp.dot(
                weights.astype(BF),
                values[:, s].reshape(total // spans, HD),
                preferred_element_type=F32,
            )
            result = sums / jnp.sum(weights, axis=1, keepdims=True)
            place = lax.broadcasted_iota(jnp.int32, (SPAN, HD), 0) + (start + s * SPAN)
            o_ref[0, s * SPAN : (s + 1) * SPAN, cols] = jnp.where(
                place < length, result, 0.0
            ).astype(BF)


def cross_attention(pos, retrieved, pick, own_w, other_w, queries, parts):
    total, enc = retrieved.shape
    half, width = own_w.shape[0], own_w.shape[1] // 2
    wide = 2 * HD
    steps = width // wide
    rows = queries.shape[1]
    whole = lambda *shape: pl.BlockSpec(shape, lambda j: (0,) * len(shape))
    key_block = pl.BlockSpec((half, wide), lambda j: (0, j))
    value_block = pl.BlockSpec((half, wide), lambda j: (0, j + steps))
    tokens = pl.BlockSpec((1, rows, wide), lambda j: (0, 0, j))
    return pl.pallas_call(
        functools.partial(cross_body, parts=parts),
        grid=(steps,),
        out_shape=jax.ShapeDtypeStruct(queries.shape, BF),
        in_specs=[
            pl.BlockSpec(memory_space=pltpu.SMEM),
            whole(total, enc),
            whole(2, enc, half),
            key_block,
            key_block,
            value_block,
            value_block,
            tokens,
        ],
        out_specs=tokens,
        scratch_shapes=[pltpu.VMEM((total, 2 * half), BF)],
        name="cross_attention",
    )(pos, retrieved, pick, own_w, other_w, own_w, other_w, queries)


def spread(x, axis):
    copies = jnp.broadcast_to(x[None], (lax.axis_size(axis),) + x.shape)
    return lax.all_to_all(copies, axis, 0, 0, tiled=True)


def local(
    queries,
    keys,
    values,
    cross_queries,
    encoded_bank,
    key_weight,
    value_weight,
    owner_ids,
    unit_ids,
    lengths,
):
    dp = ("z", "core")
    n_z, n_core, n_ctx, n_mp = (lax.axis_size(a) for a in ("z", "core", "ctx", "mp"))
    core, ctx, piece = lax.axis_index("core"), lax.axis_index("ctx"), lax.axis_index("mp")
    rows, width = queries.shape[1:]
    enc = encoded_bank.shape[3]
    asks = owner_ids.shape[1] * NBR
    part = 2 * SPAN // n_mp

    ids = jnp.concatenate([owner_ids.reshape(asks), unit_ids.reshape(asks)])
    asked = spread(ids, dp)

    shard = jnp.concatenate([key_weight, value_weight], axis=1)
    depth = shard.shape[0]
    pad = -(-depth // 8) * 8
    shard = jnp.pad(shard, ((0, pad - depth), (0, 0)))
    column = spread(shard, "z").reshape(n_z * pad, 2 * width)

    packed = lax.all_to_all(pack_heads(queries, keys, values), "ctx", 0, 0, tiled=True)
    head = self_attention(lengths, packed)
    back = lax.all_to_all(head, "ctx", 0, 0, tiled=True)
    self_core = jnp.transpose(back, (1, 0, 2)).reshape(1, rows, width)

    where = jnp.stack([lax.axis_index(dp), piece]).astype(jnp.int32)
    offered = offer_rows(asked, where, encoded_bank.reshape(-1, enc), part)
    received = lax.all_to_all(offered, dp, 0, 0, tiled=True)
    mine = choose_rows(owner_ids.reshape(asks), received).reshape(asks * part, enc)
    retrieved = lax.all_gather(mine, "mp", axis=0, tiled=True)

    own_w = spread(column, "ctx").reshape(n_ctx * n_z * pad, 2 * width)
    other_w = lax.ppermute(own_w, "core", [(i, (i + 1) % n_core) for i in range(n_core)])

    half = n_ctx * n_z * pad
    j = lax.broadcasted_iota(jnp.int32, (n_core, enc, half), 2)
    side = lax.broadcasted_iota(jnp.int32, (n_core, enc, half), 0)
    e = lax.broadcasted_iota(jnp.int32, (n_core, enc, half), 1)
    i, z, c = j % pad, (j // pad) % n_z, j // (pad * n_z)
    source = ((z * n_core + (core + side) % n_core) * n_ctx + c) * depth + i
    pick = ((source == e) & (i < depth)).astype(BF)

    pos = jnp.stack([ctx * rows, lengths[0]]).astype(jnp.int32)
    cross_core = cross_attention(pos, retrieved, pick, own_w, other_w, cross_queries, n_mp)
    return self_core, cross_core


def solution(mesh):
    n_dp, n_ctx, n_mp = (mesh.shape[a] for a in ("dp", "ctx", "mp"))
    fine = Mesh(mesh.devices.reshape(n_dp // 2, 2, n_ctx, n_mp), ("z", "core", "ctx", "mp"))
    dp = ("z", "core")
    tokens = P(dp, "ctx", "mp")
    weight = P(("z", "core", "ctx"), "mp")
    in_specs = (
        tokens,
        tokens,
        tokens,
        tokens,
        P(dp, "ctx", None, None),
        weight,
        weight,
        P(dp, "ctx", None),
        P(dp, "ctx", None),
        P(dp),
    )
    return jax.shard_map(
        local, mesh=fine, in_specs=in_specs, out_specs=(tokens, tokens), check_vma=False
    )
```

time: 930 us -> 157 us (0.17)
  waiting for transfers between devices: 853 us -> 52 us
  blocking collectives: 0 us -> 39 us
  local copies, waits for them, and re-layouts: 28.4 us -> 5.49 us
  Pallas kernels: 0 us -> 21.5 us
  starting transfers between devices: 15.2 us -> 31.3 us
  between operations: 16 us -> 1.39 us
    all_gather x4 -> x0, waiting for transfers between devices: 846 us -> none  [the longest x1 370 us: local(): lax.all_gather(value_weight, ('dp', 'ctx'), axis=0, tiled=True)]
    all_to_all x2 -> x5, waiting for transfers between devices: 5.66 us -> 52 us  [the longest x3 35.2 us: spread(): return lax.all_to_all(copies, axis, 0, 0, tiled=True)]
    all_gather x0 -> x1, blocking collectives: none -> 23.7 us  [local(): retrieved = lax.all_gather(mine, 'mp', axis=0, tiled=True)]
    pallas_call x0 -> x5, Pallas kernels: none -> 21.5 us  [the longest x1 10 us: cross_attention(): pl.pallas_call(functools.partial(cross_body, parts=parts), grid=(steps,),...]
    all_to_all x0 -> x1, blocking collectives: none -> 15.3 us  [local(): lax.all_to_all(pack_heads(queries, keys, values), 'ctx', 0, 0, tiled=True)]
    all_to_all x2 -> x5, starting transfers between devices: 15.1 us -> 29.1 us  [the longest x3 19.8 us: spread(): return lax.all_to_all(copies, axis, 0, 0, tiled=True)]
    unnamed x27 -> x9, local copies, waits for them, and re-layouts: 13.3 us -> 0.87 us
  transfers between devices with their start and end apart: 6 -> 6, of which waited for: 5 -> 4; matrix products, arithmetic and copies ran while one was open for 3% -> 3% of each run, Pallas kernels for 0% -> 7%
where the time goes in v1:
time: 157 us; the launch traced here: 155 us
  waiting for transfers between devices  52 us (33%)
  blocking collectives  39 us (25%)
  starting transfers between devices  31.3 us (20%)
  Pallas kernels  21.5 us (14%)
  local copies, waits for them, and re-layouts  5.49 us (3%)
  other arithmetic  3.85 us (2%)
    all_to_all x3, waiting for transfers between devices, spread(): return lax.all_to_all(copies, axis, 0, 0, tiled=True)  35.2 us
    all_gather x1, blocking collectives, local(): retrieved = lax.all_gather(mine, 'mp', axis=0, tiled=True)  23.7 us
    all_to_all x3, starting transfers between devices, spread(): return lax.all_to_all(copies, axis, 0, 0, tiled=True)  19.8 us
    all_to_all x1, waiting for transfers between devices, local(): received = lax.all_to_all(offered, dp, 0, 0, tiled=True)  16.9 us
    all_to_all x1, blocking collectives, local(): lax.all_to_all(pack_heads(queries, keys, values), 'ctx', 0, 0, tiled=True)  15.3 us
    pallas_call x1, Pallas kernels, cross_attention(): pl.pallas_call(functools.partial(cross_body, parts=parts), grid=(steps,),...  10 us
    all_to_all x1, starting transfers between devices, local(): back = lax.all_to_all(head, 'ctx', 0, 0, tiled=True)  5.7 us
    all_to_all x1, starting transfers between devices, local(): received = lax.all_to_all(offered, dp, 0, 0, tiled=True)  3.63 us
  transfers between devices with their start and end apart: 6, of which 4 were waited for; matrix products, arithmetic and copies ran while one was open for 3% of the time, Pallas kernels for 7%

profile of v1, /device:TPU:6, one launch (start us, length us, event | category | flops | bytes accessed | tf_op | source)
XLA Modules:
  0.0 154.5 jit_solution(15077666662077849532)
XLA Ops:
  0.6 0.8 reshape.32.own_ref
  1.4 0.0 copy-start.3
  1.4 0.8 reshape.33
  2.2 0.1 pad_add_fusion.1
  2.2 0.6 broadcast_in_dim.8
  2.8 10.4 %all-to-all-start.2 = ((s32[16,1,8]{2,1,0:T(1,128)}), s32[16,1,8]{2,1,0:T(1,128)S(1)}, u32[]{:S(2)}, u32[]{:S(2)}) async-start(s32[16,1,8]{2,1,0:T(1,128)} %broadcast_in_dim.8), calls=%async_computation.2 | async-start | bytes 16384 | tf_op jit(solution)/shard_map/all_to_all | solution.py:208
  13.3 0.8 fusion.11
  14.0 6.8 %all-to-all-done.2 = s32[16,1,8]{2,1,0:T(1,128)S(1)} async-done(((s32[16,1,8]{2,1,0:T(1,128)}), s32[16,1,8]{2,1,0:T(1,128)S(1)}, u32[]{:S(2)}, u32[]{:S(2)}) %all-to-all-start.2) | async-done | bytes 544 | tf_op jit(solution)/shard_map/all_to_all | solution.py:208
  20.8 0.0 copy-start.2
  20.8 0.7 broadcast_in_dim.9
  21.5 3.4 %all-to-all-start.4 = ((bf16[8,8,2048]{2,1,0:T(8,128)(2,1)}), bf16[8,8,2048]{2,1,0:T(8,128)(2,1)S(1)}, u32[]{:S(2)}, u32[]{:S(2)}) async-start(bf16[8,8,2048]{2,1,0:T(8,128)(2,1)} %broadcast_in_dim.9), calls=%async_computation.4 | async-start | bytes 524288 | tf_op jit(solution)/shard_map/all_to_all | solution.py:208
  24.9 2.1 %pack_heads.1 = bf16[8,3,128,128]{3,2,1,0:T(8,128)(2,1)} custom-call(bf16[1,128,1024]{2,1,0:T(8,128)(2,1)} %q_ref.2, bf16[1,128,1024]{2,1,0:T(8,128)(2,1)} %k_ref.1, bf16[1,128,1024]{2,1,0:T(8,128)(2,1)} %v_ref.1), custom_call_target="tpu_custom_call" | custom-call | tf_op jit(solution)/shard_map/pack_heads/pallas_call | solution.py:30
  27.1 9.9 %all-to-all-done.4 = bf16[8,8,2048]{2,1,0:T(8,128)(2,1)S(1)} async-done(((bf16[8,8,2048]{2,1,0:T(8,128)(2,1)}), bf16[8,8,2048]{2,1,0:T(8,128)(2,1)S(1)}, u32[]{:S(2)}, u32[]{:S(2)}) %all-to-all-start.4) | async-done | bytes 262176 | tf_op jit(solution)/shard_map/all_to_all | solution.py:208
  37.0 15.3 %all_to_all.33.x_ref = bf16[8,3,128,128]{3,2,1,0:T(8,128)(2,1)} all-to-all(bf16[8,3,128,128]{3,2,1,0:T(8,128)(2,1)} %pack_heads.1), channel_id=1, replica_groups=mesh['z'=8,'core'=2,'ctx'=8,'mp'=4] {'ctx'}, dimensions={0} | all-to-all | bytes 1572864 | tf_op jit(solution)/shard_map/all_to_all | solution.py:240
  52.4 1.6 %broadcast_in_dim.22 = bf16[8,64,2048]{2,1,0:T(8,128)(2,1)} broadcast(bf16[64,2048]{1,0:T(8,128)(2,1)S(1)} %bitcast.13), dimensions={1,2} | broadcast | bytes 2359296 | tf_op jit(solution)/shard_map/broadcast_in_dim | solution.py:207
  54.0 0.0 copy-done.3
  54.0 0.0 copy-done.2
  54.0 5.9 %all-to-all-start.5 = ((bf16[8,64,2048]{2,1,0:T(8,128)(2,1)}), bf16[8,64,2048]{2,1,0:T(8,128)(2,1)S(1)}, u32[]{:S(2)}, u32[]{:S(2)}) async-start(bf16[8,64,2048]{2,1,0:T(8,128)(2,1)} %broadcast_in_dim.22), calls=%async_computation.5 | async-start | bytes 4194304 | tf_op jit(solution)/shard_map/all_to_all | solution.py:208
  59.9 0.6 pad_add_fusion.2.where_ref
  60.5 3.6 %offer_rows.1 = bf16[16,32,896]{2,1,0:T(8,128)(2,1)} custom-call(s32[16,8]{1,0:T(8,128)} %bitcast.18, s32[2]{0:T(128)} %pad_add_fusion.2.where_ref, bf16[512,896]{1,0:T(8,128)(2,1)} %bitcast.16), custom_call_target="tpu_custom_call" | custom-call | tf_op jit(solution)/shard_map/offer_rows/pallas_call | solution.py:90
  64.1 18.4 %all-to-all-done.5 = bf16[8,64,2048]{2,1,0:T(8,128)(2,1)S(1)} async-done(((bf16[8,64,2048]{2,1,0:T(8,128)(2,1)}), bf16[8,64,2048]{2,1,0:T(8,128)(2,1)S(1)}, u32[]{:S(2)}, u32[]{:S(2)}) %all-to-all-start.5) | async-done | bytes 2097184 | tf_op jit(solution)/shard_map/all_to_all | solution.py:208
  82.5 0.0 copy-start
  82.5 3.6 %all-to-all-start.3 = ((bf16[16,32,896]{2,1,0:T(8,128)(2,1)}), bf16[16,32,896]{2,1,0:T(8,128)(2,1)S(1)}, u32[]{:S(2)}, u32[]{:S(2)}) async-start(bf16[16,32,896]{2,1,0:T(8,128)(2,1)} %offer_rows.1), calls=%async_computation.3 | async-start | bytes 1835008 | tf_op jit(solution)/shard_map/all_to_all | solution.py:247
  86.2 2.2 %collective-permute-start = (bf16[512,2048]{1,0:T(8,128)(2,1)S(1)}, bf16[512,2048]{1,0:T(8,128)(2,1)}, u32[]{:S(2)}, u32[]{:S(2)}) collective-permute-start(bf16[512,2048]{1,0:T(8,128)(2,1)S(1)} %bitcast.10), channel_id=1, source_target_pairs={{0,32},{32,0},{1,33},{33,1},{2,34},{34,2},{3,35},{35,3},{4,36},{36... | collective-permute-start | bytes 6291464 | tf_op jit(solution)/shard_map/ppermute | solution.py:252
  89.1 3.4 %self_attention.1 = bf16[8,128,128]{2,1,0:T(8,128)(2,1)} custom-call(s32[1]{0:T(128)S(6)} %copy.21.len_ref, bf16[8,3,128,128]{3,2,1,0:T(8,128)(2,1)} %all_to_all.33.x_ref), custom_call_target="tpu_custom_call" | custom-call | tf_op jit(solution)/shard_map/self_attention/pallas_call | solution.py:59
  92.6 16.9 %all-to-all-done.3.x_ref = bf16[16,32,896]{2,1,0:T(8,128)(2,1)S(1)} async-done(((bf16[16,32,896]{2,1,0:T(8,128)(2,1)}), bf16[16,32,896]{2,1,0:T(8,128)(2,1)S(1)}, u32[]{:S(2)}, u32[]{:S(2)}) %all-to-all-start.3) | async-done | bytes 917536 | tf_op jit(solution)/shard_map/all_to_all | solution.py:247
  109.4 0.0 copy-start.1
  109.4 5.7 %all-to-all-start.1 = ((bf16[8,128,128]{2,1,0:T(8,128)(2,1)}), bf16[8,128,128]{2,1,0:T(8,128)(2,1)S(1)}, u32[]{:S(2)}, u32[]{:S(2)}) async-start(bf16[8,128,128]{2,1,0:T(8,128)(2,1)} %self_attention.1), calls=%async_computation.1 | async-start | bytes 524288 | tf_op jit(solution)/shard_map/all_to_all | solution.py:242
  115.1 1.7 %fusion.8.pick_ref = bf16[2,896,512]{2,1,0:T(8,128)(2,1)} fusion(s32[512]{0:T(512)S(1)} %get-tuple-element.9, s32[512]{0:T(512)S(1)} %get-tuple-element.11, s32[512]{0:T(512)S(1)} %get-tuple-element.10, s32[512]{0:T(512)S(1)} %get-tuple-element.14, s32[2]{0:T(128)S(1)} %get-tuple-element.6, s32[2]{0:T(128)S(1)} %get-tuple-element.7, ...), kind=kLoop, calls=%fused_computation.15 | loop fusion | flops 22937600 | bytes 1848850 | tf_op jit(solution)/shard_map/convert_element_type | solution.py:260
  116.8 0.0 copy-done
  116.8 0.7 pad_add_fusion.pos_ref
  117.5 0.0 copy-done.1
  117.5 2.3 %choose_rows.1 = bf16[4,32,896]{2,1,0:T(8,128)(2,1)} custom-call(s32[4]{0:T(128)} %copy-done.3, bf16[16,32,896]{2,1,0:T(8,128)(2,1)} %copy-done.1), custom_call_target="tpu_custom_call" | custom-call | tf_op jit(solution)/shard_map/choose_rows/pallas_call | solution.py:115
  119.8 23.7 %all_gather.3.r_ref = bf16[512,896]{1,0:T(8,128)(2,1)} all-gather(bf16[128,896]{1,0:T(8,128)(2,1)} %bitcast.17), channel_id=1, replica_groups=mesh['z'=8,'core'=2,'ctx'=8,'mp'=4] {'mp'}, dimensions={0}, use_global_device_ids=true | all-gather | bytes 1146880 | tf_op jit(solution)/shard_map/all_gather | solution.py:249
  143.5 0.0 all-to-all-done.1
  143.5 0.2 copy.16
  143.7 0.9 copy.19
  144.5 0.0 collective-permute-done.kb_ref.vb_ref
  144.5 10.0 %cross_attention.1 = bf16[1,128,1024]{2,1,0:T(8,128)(2,1)} custom-call(s32[2]{0:T(128)} %pad_add_fusion.pos_ref, bf16[512,896]{1,0:T(8,128)(2,1)} %all_gather.3.r_ref, bf16[2,896,512]{2,1,0:T(8,128)(2,1)} %fusion.8.pick_ref, bf16[512,2048]{1,0:T(8,128)(2,1)} %bitcast.11, bf16[512,2048]{1,0:T(8,128)(2,1)} %collective-permute-done.kb_ref.vb_ref, ...), custom_call_target="tpu_custom_call" | custom-call | tf_op jit(solution)/shard_map/cross_attention/pallas_call | solution.py:186
  (7 shorter events, 0.1 us)
Async XLA Ops:
  1.4 52.6 %copy-start.3 = (s32[4]{0:T(128)}, s32[4]{0:T(128)S(1)}, u32[]{:S(2)}) copy-start(s32[4]{0:T(128)S(1)} %reshape.32.own_ref) | copy-start | bytes 52
  2.8 18.0 %all-to-all-start.2 = ((s32[16,1,8]{2,1,0:T(1,128)}), s32[16,1,8]{2,1,0:T(1,128)S(1)}, u32[]{:S(2)}, u32[]{:S(2)}) async-start(s32[16,1,8]{2,1,0:T(1,128)} %broadcast_in_dim.8), calls=%async_computation.2 | async-start | bytes 16384 | tf_op jit(solution)/shard_map/all_to_all | solution.py:208
  20.8 33.2 %copy-start.2 = (s32[16,1,8]{2,1,0:T(1,128)}, s32[16,1,8]{2,1,0:T(1,128)S(1)}, u32[]{:S(2)}) copy-start(s32[16,1,8]{2,1,0:T(1,128)S(1)} %all-to-all-done.2) | copy-start | bytes 1540
  21.5 15.5 %all-to-all-start.4 = ((bf16[8,8,2048]{2,1,0:T(8,128)(2,1)}), bf16[8,8,2048]{2,1,0:T(8,128)(2,1)S(1)}, u32[]{:S(2)}, u32[]{:S(2)}) async-start(bf16[8,8,2048]{2,1,0:T(8,128)(2,1)} %broadcast_in_dim.9), calls=%async_computation.4 | async-start | bytes 524288 | tf_op jit(solution)/shard_map/all_to_all | solution.py:208
  54.0 28.6 %all-to-all-start.5 = ((bf16[8,64,2048]{2,1,0:T(8,128)(2,1)}), bf16[8,64,2048]{2,1,0:T(8,128)(2,1)S(1)}, u32[]{:S(2)}, u32[]{:S(2)}) async-start(bf16[8,64,2048]{2,1,0:T(8,128)(2,1)} %broadcast_in_dim.22), calls=%async_computation.5 | async-start | bytes 4194304 | tf_op jit(solution)/shard_map/all_to_all | solution.py:208
  82.5 34.3 %copy-start = (bf16[8,64,2048]{2,1,0:T(8,128)(2,1)}, bf16[8,64,2048]{2,1,0:T(8,128)(2,1)S(1)}, u32[]{:S(2)}) copy-start(bf16[8,64,2048]{2,1,0:T(8,128)(2,1)S(1)} %all-to-all-done.5) | copy-start | bytes 6291460
  82.5 26.9 %all-to-all-start.3 = ((bf16[16,32,896]{2,1,0:T(8,128)(2,1)}), bf16[16,32,896]{2,1,0:T(8,128)(2,1)S(1)}, u32[]{:S(2)}, u32[]{:S(2)}) async-start(bf16[16,32,896]{2,1,0:T(8,128)(2,1)} %offer_rows.1), calls=%async_computation.3 | async-start | bytes 1835008 | tf_op jit(solution)/shard_map/all_to_all | solution.py:247
  86.2 58.3 %collective-permute-start = (bf16[512,2048]{1,0:T(8,128)(2,1)S(1)}, bf16[512,2048]{1,0:T(8,128)(2,1)}, u32[]{:S(2)}, u32[]{:S(2)}) collective-permute-start(bf16[512,2048]{1,0:T(8,128)(2,1)S(1)} %bitcast.10), channel_id=1, source_target_pairs={{0,32},{32,0},{1,33},{33,1},{2,34},{34,2},{3,35},{35,3},{4,36},{36... | collective-permute-start | bytes 6291464 | tf_op jit(solution)/shard_map/ppermute | solution.py:252
  109.4 8.1 %copy-start.1 = (bf16[16,32,896]{2,1,0:T(8,128)(2,1)}, bf16[16,32,896]{2,1,0:T(8,128)(2,1)S(1)}, u32[]{:S(2)}) copy-start(bf16[16,32,896]{2,1,0:T(8,128)(2,1)S(1)} %all-to-all-done.3.x_ref) | copy-start | bytes 2752516
  109.4 34.0 %all-to-all-start.1 = ((bf16[8,128,128]{2,1,0:T(8,128)(2,1)}), bf16[8,128,128]{2,1,0:T(8,128)(2,1)S(1)}, u32[]{:S(2)}, u32[]{:S(2)}) async-start(bf16[8,128,128]{2,1,0:T(8,128)(2,1)} %self_attention.1), calls=%async_computation.1 | async-start | bytes 524288 | tf_op jit(solution)/shard_map/all_to_all | solution.py:242
